TPU v7x, 512 devices: a whole 4x4x16 slice. The times are simulated.
512 devices in a mesh: rows: 64 (over x, z), cols: 8 (over y, core).
Axes of the slice: x: 4, y: 4, z: 16, core: 2. Of those that a mesh axis runs over, the one named last changes fastest.
Arguments:
- residual: float32 [3, 4096, 8192], P(None, 'rows', 'cols'), may hold values from -6 to 6
- weights: float32 [3, 4096, 8192], P(None, 'rows', 'cols'), may hold values from 0.5 to 1.5
- accumulation: bfloat16 [3, 4096, 8192], P(None, 'rows', 'cols'), may hold values from 0.19921875 to 1
- mobility: bfloat16 [3, 4096, 8192], P(None, 'rows', 'cols'), may hold values from 0.099609375 to 1
- trans: float32 [4096, 8192], P('rows', 'cols'), may hold values from 0.05 to 2
- cell_inverse: bfloat16 [9, 4096, 8192], P(None, 'rows', 'cols'), may hold values from -2.390625 to 2.390625
- pressure_inverse: bfloat16 [64, 64, 128, 128], P('rows', 'cols'), may hold values from -0.5 to 0.5
- coarse_inverse: float32 [64, 8, 8, 8], P('rows', 'cols'), may hold values from -2 to 2
- intersection_counts: int32 [64, 2], P('rows'), may hold values from 1 to 32, as said below
- slot_map: int32 [256, 64], P('rows', 'cols'), may hold values from 0 to 63
Outputs:
- update: float32 [3, 4096, 8192], P(None, 'rows', 'cols')
Inputs may be any that keep to these rules, and one draw needn't show every extreme that they name: `intersection_counts`: some entry equals 32 and some entry equals 1.
All inputs are finite; a program needn't handle non-finite values.
Results may differ from a plain program's by a relative error of at most 0.0017.
Values sent between devices are 32-bit elements; how exact they have to be, the bound alone decides.
A program may use at most 64 MiB of HBM per device.

v0:
```python
import math

import jax
import jax.numpy as jnp
from jax import lax
from jax.sharding import PartitionSpec as P

H = 32
PR = 16
PC = 128


def with_halo(cells, sides, width):
    for axis, dim in sides:
        count = lax.axis_size(axis)
        ends = count - 1
        head = lax.slice_in_dim(cells, 0, width, axis=dim)
        tail = lax.slice_in_dim(cells, cells.shape[dim] - width, cells.shape[dim], axis=dim)
        cells = jnp.concatenate(
            [
                lax.ppermute(tail, axis, [(i, (i + 1) % count) for i in range(ends)]),
                cells,
                lax.ppermute(head, axis, [((i + 1) % count, i) for i in range(ends)]),
            ],
            axis=dim,
        )
    return cells


def shards(
    residual,
    weights,
    accumulation,
    mobility,
    trans,
    cell_inverse,
    pressure_inverse,
    coarse_inverse,
    intersection_counts,
    slot_map,
):
    highest = lax.Precision.HIGHEST
    r_loc = residual.shape[1]
    c_loc = residual.shape[2]
    margin = H
    ext_rows = r_loc + 2 * margin
    groups = pressure_inverse.shape[1]
    width = c_loc // groups
    rp_own = jnp.sum(residual * weights, axis=0)
    rp_ext = with_halo(rp_own, (("rows", 0),), margin)
    counts = intersection_counts[0]
    e_index = jnp.arange(ext_rows, dtype=jnp.int32)
    keep = ((e_index >= margin - counts[0]) & (e_index < r_loc + margin + counts[1])).astype(
        jnp.float32
    )
    ext_b = (rp_ext * keep[:, None]).astype(jnp.bfloat16)
    z_ext = jnp.einsum(
        "bij,jbg->ibg",
        pressure_inverse[0],
        ext_b.reshape(ext_rows, groups, width),
        preferred_element_type=jnp.float32,
    )
    z_part = z_ext.reshape(ext_rows, c_loc)[margin : margin + r_loc]
    kmax = coarse_inverse.shape[-1]
    owners = lax.axis_size("cols")
    slots = owners * kmax
    npr = r_loc // PR
    npc = c_loc // PC
    psum = rp_own.reshape(npr, PR, npc, PC).sum(axis=(1, 3)) * (1.0 / math.sqrt(PR * PC))
    onehot = (slot_map[:, :, None] == jnp.arange(slots, dtype=jnp.int32)).astype(jnp.float32)
    partial_tiles = jnp.einsum("pq,pqk->k", psum, onehot, precision=highest)
    owned = lax.psum_scatter(partial_tiles, "cols", scatter_dimension=0, tiled=True)
    solved = jnp.dot(coarse_inverse[0, 0], owned, precision=highest)
    coarse = lax.all_gather(solved, "cols", axis=0, tiled=True)
    patch_corr = jnp.einsum("pqk,k->pq", onehot, coarse, precision=highest)
    cell_corr = jnp.broadcast_to(patch_corr[:, None, :, None], (npr, PR, npc, PC)).reshape(
        r_loc, c_loc
    )
    dp = z_part + cell_corr
    pair = jnp.stack([dp, trans], axis=0)
    rimmed = with_halo(pair, (("rows", 1), ("cols", 2)), 1)
    dpad = rimmed[0]
    tpad = rimmed[1]
    flux = jnp.zeros((r_loc, c_loc), jnp.float32)
    for near_t, near_d in (
        (tpad[2:, 1:-1], dpad[2:, 1:-1]),
        (tpad[:-2, 1:-1], dpad[:-2, 1:-1]),
        (tpad[1:-1, 2:], dpad[1:-1, 2:]),
        (tpad[1:-1, :-2], dpad[1:-1, :-2]),
    ):
        flux = flux + 2.0 * trans * near_t / (trans + near_t) * (dp - near_d)
    r_two = residual - (
        accumulation.astype(jnp.float32) * dp[None] + mobility.astype(jnp.float32) * flux[None]
    )
    blocks = cell_inverse.astype(jnp.float32).reshape(3, 3, r_loc, c_loc)
    update = jnp.sum(blocks * r_two[None], axis=1)
    update = update.at[0].add(dp)
    return update


def solution(mesh):
    in_specs = (
        P(None, "rows", "cols"),
        P(None, "rows", "cols"),
        P(None, "rows", "cols"),
        P(None, "rows", "cols"),
        P("rows", "cols"),
        P(None, "rows", "cols"),
        P("rows", "cols", None, None),
        P("rows", "cols", None, None),
        P("rows", None),
        P("rows", "cols"),
    )
    out_specs = P(None, "rows", "cols")
    return jax.shard_map(shards, mesh=mesh, in_specs=in_specs, out_specs=out_specs, check_vma=False)
```

profile of v0, /device:TPU:14, one launch (start us, length us, event | category | flops | bytes accessed | tf_op | source)
XLA Modules:
  0.0 70.5 jit_solution(7937370686991783078)
XLA Ops:
  0.0 0.0 copy-start
  0.0 0.0 copy-start.6
  0.0 1.5 %multiply_reduce_fusion = f32[64,1024]{1,0:T(8,128)S(1)} fusion(f32[3,64,1024]{2,1,0:T(8,128)} %param.12, f32[3,64,1024]{2,1,0:T(8,128)} %param.13), kind=kLoop, calls=%fused_computation.6 | loop fusion | flops 327680 | bytes 1835008 | tf_op jit(solution)/shard_map/reduce_sum | solution.py:49
  1.6 0.0 copy-start.7
  1.6 3.8 %collective-permute-start = (f32[32,1024]{1,0:T(8,128)S(1)}, f32[32,1024]{1,0:T(8,128)S(1)}, u32[]{:S(2)}, u32[]{:S(2)}) collective-permute-start(f32[32,1024]{1,0:T(8,128)S(1)} %get-tuple-element.27), channel_id=1, source_target_pairs={{0,8},{8,16},{16,24},{24,32},{32,40},{40,48},{48,56},{56,64},{64,7... | collective-permute-start | bytes 393224 | tf_op jit(solution)/shard_map/ppermute | solution.py:21
  5.4 9.8 %collective-permute-start.1 = (f32[32,1024]{1,0:T(8,128)S(1)}, f32[32,1024]{1,0:T(8,128)S(1)}, u32[]{:S(2)}, u32[]{:S(2)}) collective-permute-start(f32[32,1024]{1,0:T(8,128)S(1)} %get-tuple-element.28), channel_id=1, source_target_pairs={{8,0},{16,8},{24,16},{32,24},{40,32},{48,40},{56,48},{64,56},{72,6... | collective-permute-start | bytes 393224 | tf_op jit(solution)/shard_map/ppermute | solution.py:23
  15.3 0.1 bitcast_reduce_fusion
  15.4 0.0 copy-done.9
  15.4 0.2 convolution_bitcast_fusion.1
  15.6 11.5 %all-reduce.1 = f32[64]{0:T(128)S(1)} all-reduce(f32[64]{0:T(128)S(1)} %convolution_bitcast_fusion.1), channel_id=2, replica_groups=mesh['rows'=64,'cols'=8] {'cols'}, use_global_device_ids=true, to_apply=%region_2.0.clone | all-reduce | flops 64 | bytes 512
  27.1 0.0 copy-done.8
  27.1 0.6 fusion.21
  29.1 0.0 copy-done.6
  29.1 0.2 convolution_bitcast_fusion.2
  29.3 0.2 dynamic-update-slice.3
  29.5 12.4 %all-reduce = f32[64]{0:T(128)S(1)} all-reduce(f32[64]{0:T(128)S(1)} %dynamic-update-slice.3), channel_id=1, replica_groups=mesh['rows'=64,'cols'=8] {'cols'}, use_global_device_ids=true, to_apply=%add | all-reduce | flops 64 | bytes 512
  41.9 0.3 fusion.14
  42.2 0.6 fusion.22
  42.8 0.1 broadcast_in_dim.2
  44.2 0.0 collective-permute-done
  44.3 0.0 collective-permute-done.1
  44.3 0.2 fusion.1
  44.5 0.2 convolution_bitcast_fusion
  44.8 0.0 copy-start.2
  44.8 0.2 copy.15
  45.1 0.6 copy-done.2
  45.7 1.9 %collective-permute-start.2 = (f32[2,1,1024]{2,1,0:T(1,128)S(1)}, f32[2,1,1024]{2,1,0:T(1,128)S(1)}, u32[]{:S(2)}, u32[]{:S(2)}) collective-permute-start(f32[2,1,1024]{2,1,0:T(1,128)S(1)} %get-tuple-element.25), channel_id=1, source_target_pairs={{0,8},{8,16},{16,24},{24,32},{32,40},{40,48},{48,56},{56,64},{64,7... | collective-permute-start | bytes 24584 | tf_op jit(solution)/shard_map/ppermute | solution.py:21
  47.7 6.0 %collective-permute-start.3 = (f32[2,1,1024]{2,1,0:T(1,128)S(1)}, f32[2,1,1024]{2,1,0:T(1,128)S(1)}, u32[]{:S(2)}, u32[]{:S(2)}) collective-permute-start(f32[2,1,1024]{2,1,0:T(1,128)S(1)} %get-tuple-element.26), channel_id=1, source_target_pairs={{8,0},{16,8},{24,16},{32,24},{40,32},{48,40},{56,48},{64,56},{72,6... | collective-permute-start | bytes 24584 | tf_op jit(solution)/shard_map/ppermute | solution.py:23
  53.7 0.0 collective-permute-done.2
  53.7 1.3 %collective-permute-done.3 = f32[2,1,1024]{2,1,0:T(1,128)S(1)} collective-permute-done((f32[2,1,1024]{2,1,0:T(1,128)S(1)}, f32[2,1,1024]{2,1,0:T(1,128)S(1)}, u32[]{:S(2)}, u32[]{:S(2)}) %collective-permute-start.3) | collective-permute-done | bytes 8224 | tf_op jit(solution)/shard_map/ppermute | solution.py:23
  55.0 0.1 pad_maximum_fusion
  55.1 0.1 fusion.19
  55.2 3.7 %collective-permute-start.5 = (f32[2,66,1]{2,1,0:T(8,128)S(1)}, f32[2,66,1]{2,1,0:T(8,128)S(1)}, u32[]{:S(2)}, u32[]{:S(2)}) collective-permute-start(f32[2,66,1]{2,1,0:T(8,128)S(1)} %get-tuple-element.21), channel_id=1, source_target_pairs={{1,0},{2,1},{3,2},{4,3},{5,4},{6,5},{7,6},{9,8},{10,9},{11,10},{12... | collective-permute-start | bytes 1592 | tf_op jit(solution)/shard_map/ppermute | solution.py:23
  58.9 1.9 %collective-permute-start.4 = (f32[2,66,1]{2,1,0:T(8,128)S(1)}, f32[2,66,1]{2,1,0:T(8,128)S(1)}, u32[]{:S(2)}, u32[]{:S(2)}) collective-permute-start(f32[2,66,1]{2,1,0:T(8,128)S(1)} %get-tuple-element.22), channel_id=1, source_target_pairs={{0,1},{1,2},{2,3},{3,4},{4,5},{5,6},{6,7},{8,9},{9,10},{10,11},{11... | collective-permute-start | bytes 1592 | tf_op jit(solution)/shard_map/ppermute | solution.py:21
  60.9 0.0 collective-permute-done.5
  60.9 3.8 %collective-permute-done.4 = f32[2,66,1]{2,1,0:T(8,128)S(1)} collective-permute-done((f32[2,66,1]{2,1,0:T(8,128)S(1)}, f32[2,66,1]{2,1,0:T(8,128)S(1)}, u32[]{:S(2)}, u32[]{:S(2)}) %collective-permute-start.4) | collective-permute-done | bytes 560 | tf_op jit(solution)/shard_map/ppermute | solution.py:21
  64.6 0.4 concatenate.23
  65.1 0.0 copy-start.1
  65.1 0.0 copy-start.4
  65.1 0.0 copy-start.5
  65.1 0.6 fusion.4
  65.7 0.5 copy-done.1
  66.2 0.1 copy-done.4
  66.3 0.1 copy-done.5
  66.4 0.2 add_subtract_fusion
  66.6 1.1 %copy-done.3 = bf16[9,64,1024]{2,1,0:T(8,128)(2,1)S(1)} copy-done((bf16[9,64,1024]{2,1,0:T(8,128)(2,1)S(1)}, bf16[9,64,1024]{2,1,0:T(8,128)(2,1)}, u32[]{:S(2)}) %copy-start.3) | copy-done | bytes 1179672
  67.7 1.1 %fusion = f32[3,64,1024]{2,1,0:T(8,128)} fusion(bf16[3,3,64,1024]{3,2,1,0:T(8,128)(2,1)S(1)} %bitcast.64, f32[3,64,1024]{2,1,0:T(8,128)S(1)} %add_subtract_fusion), kind=kLoop, calls=%fused_computation.1 | loop fusion | flops 1572864 | bytes 2752512 | tf_op jit(solution)/shard_map/reduce_sum | solution.py:96
  68.8 1.7 %fusion.2 = f32[3,64,1024]{2,1,0:T(8,128)} fusion(f32[3,64,1024]{2,1,0:T(8,128)} %fusion, f32[1,64,1024]{2,1,0:T(8,128)S(1)} %add.48), kind=kLoop, calls=%fused_computation.15 | loop fusion | flops 65536 | bytes 786432 | tf_op jit(solution)/shard_map/scatter-add | solution.py:97
  (18 shorter events, 0.4 us)
Async XLA Ops:
  0.0 44.5 %copy-start = (bf16[1,8,128,128]{3,2,1,0:T(8,128)(2,1)S(1)}, bf16[1,8,128,128]{3,2,1,0:T(8,128)(2,1)}, u32[]{:S(2)}) copy-start(bf16[1,8,128,128]{3,2,1,0:T(8,128)(2,1)} %param.18) | copy-start | bytes 786436
  0.0 27.1 %copy-start.8 = (u32[512]{0:T(512)S(1)}, u32[512]{0:T(512)}, u32[]{:S(2)}) copy-start(u32[512]{0:T(512)} %constant.45) | copy-start | bytes 6148
  0.0 15.4 %copy-start.9 = (s32[4,8]{1,0:T(4,128)S(1)}, s32[4,8]{1,0:T(4,128)}, u32[]{:S(2)}) copy-start(s32[4,8]{1,0:T(4,128)} %param.21) | copy-start | bytes 388
  0.0 29.1 %copy-start.6 = (f32[1,1,8,8]{3,2,1,0:T(8,128)S(1)}, f32[1,1,8,8]{3,2,1,0:T(8,128)}, u32[]{:S(2)}) copy-start(f32[1,1,8,8]{3,2,1,0:T(8,128)} %param.19) | copy-start | bytes 772
  1.6 40.6 %copy-start.7 = (s32[1,2]{1,0:T(1,128)S(1)}, s32[1,2]{1,0:T(1,128)}, u32[]{:S(2)}) copy-start(s32[1,2]{1,0:T(1,128)} %param.20) | copy-start | bytes 28
  1.6 42.6 %collective-permute-start = (f32[32,1024]{1,0:T(8,128)S(1)}, f32[32,1024]{1,0:T(8,128)S(1)}, u32[]{:S(2)}, u32[]{:S(2)}) collective-permute-start(f32[32,1024]{1,0:T(8,128)S(1)} %get-tuple-element.27), channel_id=1, source_target_pairs={{0,8},{8,16},{16,24},{24,32},{32,40},{40,48},{48,56},{56,64},{64,7... | collective-permute-start | bytes 393224 | tf_op jit(solution)/shard_map/ppermute | solution.py:21
  5.4 38.8 %collective-permute-start.1 = (f32[32,1024]{1,0:T(8,128)S(1)}, f32[32,1024]{1,0:T(8,128)S(1)}, u32[]{:S(2)}, u32[]{:S(2)}) collective-permute-start(f32[32,1024]{1,0:T(8,128)S(1)} %get-tuple-element.28), channel_id=1, source_target_pairs={{8,0},{16,8},{24,16},{32,24},{40,32},{48,40},{56,48},{64,56},{72,6... | collective-permute-start | bytes 393224 | tf_op jit(solution)/shard_map/ppermute | solution.py:23
  44.8 1.0 %copy-start.2 = (f32[64,1024]{1,0:T(8,128)S(1)}, f32[64,1024]{1,0:T(8,128)}, u32[]{:S(2)}) copy-start(f32[64,1024]{1,0:T(8,128)} %param.16) | copy-start | bytes 786436
  45.7 8.0 %collective-permute-start.2 = (f32[2,1,1024]{2,1,0:T(1,128)S(1)}, f32[2,1,1024]{2,1,0:T(1,128)S(1)}, u32[]{:S(2)}, u32[]{:S(2)}) collective-permute-start(f32[2,1,1024]{2,1,0:T(1,128)S(1)} %get-tuple-element.25), channel_id=1, source_target_pairs={{0,8},{8,16},{16,24},{24,32},{32,40},{40,48},{48,56},{56,64},{64,7... | collective-permute-start | bytes 24584 | tf_op jit(solution)/shard_map/ppermute | solution.py:21
  47.7 7.4 %collective-permute-start.3 = (f32[2,1,1024]{2,1,0:T(1,128)S(1)}, f32[2,1,1024]{2,1,0:T(1,128)S(1)}, u32[]{:S(2)}, u32[]{:S(2)}) collective-permute-start(f32[2,1,1024]{2,1,0:T(1,128)S(1)} %get-tuple-element.26), channel_id=1, source_target_pairs={{8,0},{16,8},{24,16},{32,24},{40,32},{48,40},{56,48},{64,56},{72,6... | collective-permute-start | bytes 24584 | tf_op jit(solution)/shard_map/ppermute | solution.py:23
  55.2 5.7 %collective-permute-start.5 = (f32[2,66,1]{2,1,0:T(8,128)S(1)}, f32[2,66,1]{2,1,0:T(8,128)S(1)}, u32[]{:S(2)}, u32[]{:S(2)}) collective-permute-start(f32[2,66,1]{2,1,0:T(8,128)S(1)} %get-tuple-element.21), channel_id=1, source_target_pairs={{1,0},{2,1},{3,2},{4,3},{5,4},{6,5},{7,6},{9,8},{10,9},{11,10},{12... | collective-permute-start | bytes 1592 | tf_op jit(solution)/shard_map/ppermute | solution.py:23
  58.9 5.7 %collective-permute-start.4 = (f32[2,66,1]{2,1,0:T(8,128)S(1)}, f32[2,66,1]{2,1,0:T(8,128)S(1)}, u32[]{:S(2)}, u32[]{:S(2)}) collective-permute-start(f32[2,66,1]{2,1,0:T(8,128)S(1)} %get-tuple-element.22), channel_id=1, source_target_pairs={{0,1},{1,2},{2,3},{3,4},{4,5},{5,6},{6,7},{8,9},{9,10},{10,11},{11... | collective-permute-start | bytes 1592 | tf_op jit(solution)/shard_map/ppermute | solution.py:21
  65.1 1.1 %copy-start.1 = (f32[3,64,1024]{2,1,0:T(8,128)S(1)}, f32[3,64,1024]{2,1,0:T(8,128)}, u32[]{:S(2)}) copy-start(f32[3,64,1024]{2,1,0:T(8,128)} %param.12) | copy-start | bytes 2359300
  65.1 1.2 %copy-start.4 = (bf16[3,64,1024]{2,1,0:T(8,128)(2,1)S(1)}, bf16[3,64,1024]{2,1,0:T(8,128)(2,1)}, u32[]{:S(2)}) copy-start(bf16[3,64,1024]{2,1,0:T(8,128)(2,1)} %param.15) | copy-start | bytes 1179652
  65.1 1.3 %copy-start.5 = (bf16[3,64,1024]{2,1,0:T(8,128)(2,1)S(1)}, bf16[3,64,1024]{2,1,0:T(8,128)(2,1)}, u32[]{:S(2)}) copy-start(bf16[3,64,1024]{2,1,0:T(8,128)(2,1)} %param.14) | copy-start | bytes 1179652
  66.4 1.3 %copy-start.3 = (bf16[9,64,1024]{2,1,0:T(8,128)(2,1)S(1)}, bf16[9,64,1024]{2,1,0:T(8,128)(2,1)}, u32[]{:S(2)}) copy-start(bf16[9,64,1024]{2,1,0:T(8,128)(2,1)} %param.17) | copy-start | bytes 3538948
where the time goes:
time: 71 us; the launch traced here: 70.5 us
  starting transfers between devices  27.2 us (38%)
  blocking collectives  23.9 us (34%)
  other arithmetic  5.56 us (8%)
  waiting for transfers between devices  5.13 us (7%)
  local copies, waits for them, and re-layouts  4.96 us (7%)
  between operations  2.84 us (4%)
  matrix products  0.9 us (1%)
    unnamed x2, blocking collectives  23.9 us
    ppermute x3, starting transfers between devices, with_halo(): lax.ppermute(head, axis, [((i + 1) % count, i) for i in range(ends)])  19.5 us
    ppermute x3, starting transfers between devices, with_halo(): lax.ppermute(tail, axis, [(i, (i + 1) % count) for i in range(ends)])  7.67 us
    ppermute x3, waiting for transfers between devices, with_halo(): lax.ppermute(tail, axis, [(i, (i + 1) % count) for i in range(ends)])  3.76 us
    unnamed x27, local copies, waits for them, and re-layouts  3.46 us
    scatter-add x1, other arithmetic, shards(): update = update.at[0].add(dp)  1.68 us
    reduce_sum x1, other arithmetic, shards(): rp_own = jnp.sum(residual * weights, axis=0)  1.54 us
  transfers between devices with their start and end apart: 6, of which 2 were waited for; matrix products, arithmetic and copies ran while one was open for 4% of the time, Pallas kernels for 0%

commit v1 on v0

v1 whole, which is shorter than its diff:
```python
import functools
import math

import jax
import jax.numpy as jnp
from jax import lax
from jax.experimental import pallas as pl
from jax.experimental.pallas import tpu as pltpu
from jax.sharding import PartitionSpec as P

H = 32
PR = 16
PC = 128
L = 128
TOP = 8
MESH = pl.DeviceIdType.MESH
F32 = jnp.float32
BF16 = jnp.bfloat16


def kernel(
    nr, nc,
    res_h, wts_h, acc_h, mob_h, trans_h, cell_h, pinv_h, ci_ref, cnt_ref, slot_ref,
    out_ref,
    res_v, wts_v, acc_v, mob_v, tp_v, cell_v, pinv_v,
    rp_v, halo_v, ext_v, trow_s, trow_r, tcol_r, drow_s, drow_r, dcol_r, dp_v, cv_v, ch_v,
    ps_v, tile_s, tile_r, corr_v,
    load_sem, send_sem, recv_sem, tile_send, tile_recv,
):
    rows = trans_h.shape[0]
    cols = trans_h.shape[1]
    nq = cols // L
    npr = rows // PR
    kmax = ci_ref.shape[-1]
    me_r = lax.axis_index("rows")
    me_c = lax.axis_index("cols")
    up = lax.rem(me_r + 1, nr)
    down = lax.rem(me_r + nr - 1, nr)
    right = lax.rem(me_c + 1, nc)
    left = lax.rem(me_c + nc - 1, nc)

    def load(src, dst, i):
        copy = pltpu.make_async_copy(src, dst, load_sem.at[i])
        copy.start()
        return copy

    rw = []
    for half in range(2):
        span = pl.ds(half * H, H)
        rw.append((
            load(res_h.at[:, span, :], res_v.at[:, span, :], 2 * half),
            load(wts_h.at[:, span, :], wts_v.at[:, span, :], 2 * half + 1),
        ))
    load_t = load(trans_h, tp_v.at[pl.ds(TOP, rows), :], 4)
    load_p = load(pinv_h.at[0], pinv_v, 5)
    load_a = load(acc_h, acc_v, 6)
    load_m = load(mob_h, mob_v, 7)
    load_c = load(cell_h, cell_v, 8)

    barrier = pltpu.get_barrier_semaphore()
    for target in (up, down):
        pl.semaphore_signal(barrier, inc=1, device_id=(target, me_c), device_id_type=MESH)
    for k in range(1, nc):
        pl.semaphore_signal(
            barrier, inc=1, device_id=(me_r, lax.rem(me_c + k, nc)), device_id_type=MESH
        )

    def send(src, dst, i, device):
        copy = pltpu.make_async_remote_copy(
            src_ref=src, dst_ref=dst, send_sem=send_sem.at[i], recv_sem=recv_sem.at[i],
            device_id=device, device_id_type=MESH,
        )
        copy.start()
        return copy

    lane8 = lax.broadcasted_iota(jnp.int32, (8, L), 1)
    block = jnp.zeros((kmax, L), F32)
    own = ci_ref[0, 0]
    for j in range(kmax):
        block = block + jnp.where(lane8 == me_c * kmax + j, own[:, j : j + 1], 0.0)
    tile_s[0:8, :] = block
    tile_s[8:16, :] = jnp.zeros((8, L), F32)

    row_e = lax.broadcasted_iota(jnp.int32, (H, L), 0)
    lo_count = jnp.where(me_r > 0, cnt_ref[0, 0], 0)
    hi_count = jnp.where(me_r < nr - 1, cnt_ref[0, 1], 0)

    halos = []
    for half in range(2):
        rw[half][0].wait()
        rw[half][1].wait()
        for p in range(half * H // PR, (half + 1) * H // PR):
            r = slice(p * PR, (p + 1) * PR)
            for q in range(nq):
                c = slice(q * L, (q + 1) * L)
                rp = res_v[0, r, c] * wts_v[0, r, c]
                rp = rp + res_v[1, r, c] * wts_v[1, r, c]
                rp = rp + res_v[2, r, c] * wts_v[2, r, c]
                rp_v[r, c] = rp
                ext_v[H + p * PR : H + (p + 1) * PR, c] = rp.astype(BF16)
                ps_v[p : p + 1, c] = jnp.sum(rp, axis=0, keepdims=True)
        if half == 0:
            pl.semaphore_wait(barrier, nc + 1)
            halos.append(send(rp_v.at[pl.ds(0, H), :], halo_v.at[1], 0, (down, me_c)))
        else:
            halos.append(send(rp_v.at[pl.ds(H, H), :], halo_v.at[0], 1, (up, me_c)))

    lane4 = lax.broadcasted_iota(jnp.int32, (npr, L), 1)
    slots = slot_ref[...]
    tiles = jnp.zeros((npr, L), F32)
    hot = []
    for q in range(nq):
        sums = jnp.sum(ps_v[0:npr, q * L : (q + 1) * L], axis=1, keepdims=True)
        hit = lane4 == slots[:, q : q + 1]
        hot.append(hit)
        tiles = tiles + jnp.where(hit, sums, 0.0)
    tiles = jnp.sum(tiles, axis=0, keepdims=True) * (1.0 / math.sqrt(PR * PC))
    tile_s[8:9, :] = tiles
    tile_copies = []
    for k in range(1, nc):
        copy = pltpu.make_async_remote_copy(
            src_ref=tile_s, dst_ref=tile_r.at[k],
            send_sem=tile_send.at[k], recv_sem=tile_recv.at[k],
            device_id=(me_r, lax.rem(me_c + k, nc)), device_id_type=MESH,
        )
        copy.start()
        tile_copies.append(copy)

    load_t.wait()
    trow_s[0] = tp_v[TOP : TOP + 1, :]
    trow_s[1] = tp_v[TOP + rows - 1 : TOP + rows, :]
    body = pl.ds(TOP, rows)
    first = pl.ds(0, L)
    last = pl.ds(cols - L, L)
    edge_t = [
        send(trow_s.at[0], trow_r.at[1], 2, (down, me_c)),
        send(trow_s.at[1], trow_r.at[0], 3, (up, me_c)),
        send(tp_v.at[body, first], tcol_r.at[1], 4, (me_r, left)),
        send(tp_v.at[body, last], tcol_r.at[0], 5, (me_r, right)),
    ]
    for copy in edge_t:
        copy.wait()
    tp_v[TOP - 1 : TOP, :] = trow_r[0]
    tp_v[TOP + rows : TOP + rows + 1, :] = trow_r[1]

    lane16 = lax.broadcasted_iota(jnp.int32, (PR, L), 1)
    is_last = lane16 == L - 1
    is_first = lane16 == 0

    def mean(a, b):
        return 2.0 * a * b / (a + b)

    for q in range(nq):
        c = slice(q * L, (q + 1) * L)
        low = mean(tp_v[TOP - 1 : TOP, c], tp_v[TOP : TOP + 1, c])
        cv_v[TOP - 1 : TOP, c] = jnp.where(me_r > 0, low, 0.0)
    for p in range(npr):
        r0 = TOP + p * PR
        blocks = [tcol_r[0, p * PR : (p + 1) * PR, :]]
        blocks += [tp_v[r0 : r0 + PR, q * L : (q + 1) * L] for q in range(nq)]
        blocks += [tcol_r[1, p * PR : (p + 1) * PR, :]]
        turned = [pltpu.roll(b, L - 1, 1) for b in blocks[1:]]
        for q in range(nq + 1):
            here = blocks[q]
            if q == 0:
                near = turned[0]
            else:
                near = jnp.where(is_last, turned[q], turned[q - 1])
            face = mean(here, near)
            if q == 0:
                face = jnp.where(me_c > 0, face, 0.0)
            if q == nq:
                face = jnp.where(is_last & (me_c == nc - 1), 0.0, face)
            ch_v[p * PR : (p + 1) * PR, q * L : (q + 1) * L] = face
            if q > 0:
                c = slice((q - 1) * L, q * L)
                cv_v[r0 : r0 + PR, c] = mean(here, tp_v[r0 + 1 : r0 + PR + 1, c])
    for q in range(nq):
        c = slice(q * L, (q + 1) * L)
        r = slice(TOP + rows - 1, TOP + rows)
        cv_v[r, c] = jnp.where(me_r < nr - 1, cv_v[r, c], 0.0)

    for copy in tile_copies:
        copy.wait()
    total = tile_s[8:16, :]
    for k in range(1, nc):
        total = total + tile_r[k, 8:16, :]
    total = total[0:1, :]
    sub8 = lax.broadcasted_iota(jnp.int32, (8, L), 0)
    coarse = jnp.zeros((8, L), F32)
    for k in range(nc):
        part = tile_s[0:8, :] if k == 0 else tile_r[k, 0:8, :]
        owner = lax.rem(me_c - k + nc, nc)
        value = jnp.sum(part * total, axis=1, keepdims=True)
        coarse = coarse + jnp.where(lane8 == owner * kmax + sub8, value, 0.0)
    coarse = jnp.sum(coarse, axis=0, keepdims=True)
    for q in range(nq):
        corr = jnp.sum(jnp.where(hot[q], coarse, 0.0), axis=1, keepdims=True)
        corr_v[0:npr, q * L : (q + 1) * L] = jnp.broadcast_to(corr, (npr, L))

    load_p.wait()
    for copy in halos:
        copy.wait()
    for q in range(nq):
        c = slice(q * L, (q + 1) * L)
        low = jnp.where(row_e >= H - lo_count, halo_v[0, :, c], 0.0)
        high = jnp.where(row_e < hi_count, halo_v[1, :, c], 0.0)
        ext_v[0:H, c] = low.astype(BF16)
        ext_v[H + rows : 2 * H + rows, c] = high.astype(BF16)
        z = jnp.dot(pinv_v[q, H : H + rows, :], ext_v[:, c], preferred_element_type=F32)
        for p in range(npr):
            dp = z[p * PR : (p + 1) * PR, :] + corr_v[p : p + 1, c]
            dp_v[TOP + p * PR : TOP + (p + 1) * PR, c] = dp
            if p == 0:
                drow_s[0, :, c] = dp[0:1, :]
            if p == npr - 1:
                drow_s[1, :, c] = dp[PR - 1 : PR, :]
    edge_d = [
        send(drow_s.at[0], drow_r.at[1], 6, (down, me_c)),
        send(drow_s.at[1], drow_r.at[0], 7, (up, me_c)),
        send(dp_v.at[body, first], dcol_r.at[1], 8, (me_r, left)),
        send(dp_v.at[body, last], dcol_r.at[0], 9, (me_r, right)),
    ]
    load_a.wait()
    load_m.wait()
    load_c.wait()
    for copy in edge_d:
        copy.wait()
    dp_v[TOP - 1 : TOP, :] = drow_r[0]
    dp_v[TOP + rows : TOP + rows + 1, :] = drow_r[1]

    for p in range(npr):
        r0 = TOP + p * PR
        r = slice(p * PR, (p + 1) * PR)
        blocks = [dcol_r[0, r, :]]
        blocks += [dp_v[r0 : r0 + PR, q * L : (q + 1) * L] for q in range(nq)]
        blocks += [dcol_r[1, r, :]]
        turned = [pltpu.roll(b, L - 1, 1) for b in blocks[1:]]
        before = None
        for q in range(nq + 1):
            here = blocks[q]
            if q == 0:
                near = turned[0]
            else:
                near = jnp.where(is_last, turned[q], turned[q - 1])
            face = ch_v[r, q * L : (q + 1) * L] * (here - near)
            moved = pltpu.roll(face, 1, 1)
            if q > 0:
                c = slice((q - 1) * L, q * L)
                flux = face - jnp.where(is_first, before, moved)
                flux = flux + cv_v[r0 : r0 + PR, c] * (here - dp_v[r0 + 1 : r0 + PR + 1, c])
                flux = flux + cv_v[r0 - 1 : r0 + PR - 1, c] * (here - dp_v[r0 - 1 : r0 + PR - 1, c])
                r2 = [
                    res_v[k, r, c]
                    - (acc_v[k, r, c].astype(F32) * here + mob_v[k, r, c].astype(F32) * flux)
                    for k in range(3)
                ]
                for k in range(3):
                    u = cell_v[3 * k, r, c].astype(F32) * r2[0]
                    u = u + cell_v[3 * k + 1, r, c].astype(F32) * r2[1]
                    u = u + cell_v[3 * k + 2, r, c].astype(F32) * r2[2]
                    if k == 0:
                        u = u + here
                    out_ref[k, r, c] = u
            before = moved


def shards(nr, nc, *args):
    residual, pinv = args[0], args[6]
    rows, cols = residual.shape[1:]
    groups = pinv.shape[1]
    e = rows + 2 * H
    hbm = pl.BlockSpec(memory_space=pl.ANY)
    vmem = pl.BlockSpec(memory_space=pltpu.VMEM)
    smem = pl.BlockSpec(memory_space=pltpu.SMEM)
    tall = rows + 2 * TOP
    scratch = [
        pltpu.VMEM((3, rows, cols), F32),
        pltpu.VMEM((3, rows, cols), F32),
        pltpu.VMEM((3, rows, cols), BF16),
        pltpu.VMEM((3, rows, cols), BF16),
        pltpu.VMEM((tall, cols), F32),
        pltpu.VMEM((9, rows, cols), BF16),
        pltpu.VMEM((groups, e, L), BF16),
        pltpu.VMEM((rows, cols), F32),
        pltpu.VMEM((2, H, cols), F32),
        pltpu.VMEM((e, cols), BF16),
        pltpu.VMEM((2, 1, cols), F32),
        pltpu.VMEM((2, 1, cols), F32),
        pltpu.VMEM((2, rows, L), F32),
        pltpu.VMEM((2, 1, cols), F32),
        pltpu.VMEM((2, 1, cols), F32),
        pltpu.VMEM((2, rows, L), F32),
        pltpu.VMEM((tall, cols), F32),
        pltpu.VMEM((tall, cols), F32),
        pltpu.VMEM((rows, cols + L), F32),
        pltpu.VMEM((8, cols), F32),
        pltpu.VMEM((16, L), F32),
        pltpu.VMEM((nc, 16, L), F32),
        pltpu.VMEM((8, cols), F32),
        pltpu.SemaphoreType.DMA((9,)),
        pltpu.SemaphoreType.DMA((10,)),
        pltpu.SemaphoreType.DMA((10,)),
        pltpu.SemaphoreType.DMA((nc,)),
        pltpu.SemaphoreType.DMA((nc,)),
    ]
    return pl.pallas_call(
        functools.partial(kernel, nr, nc),
        out_shape=jax.ShapeDtypeStruct((3, rows, cols), F32),
        in_specs=[hbm] * 7 + [vmem, smem, vmem],
        out_specs=vmem,
        scratch_shapes=scratch,
        compiler_params=pltpu.CompilerParams(
            collective_id=0, has_side_effects=True, vmem_limit_bytes=60 * 1024 * 1024
        ),
    )(*args)


def solution(mesh):
    in_specs = (
        P(None, "rows", "cols"),
        P(None, "rows", "cols"),
        P(None, "rows", "cols"),
        P(None, "rows", "cols"),
        P("rows", "cols"),
        P(None, "rows", "cols"),
        P("rows", "cols", None, None),
        P("rows", "cols", None, None),
        P("rows", None),
        P("rows", "cols"),
    )
    out_specs = P(None, "rows", "cols")
    body = functools.partial(shards, mesh.shape["rows"], mesh.shape["cols"])
    return jax.shard_map(body, mesh=mesh, in_specs=in_specs, out_specs=out_specs, check_vma=False)
```

time: 71 us -> 29 us (0.41)
  the two profiles are of different devices: /device:TPU:14 before, /device:TPU:1 now
where the time goes in v1:
time: 29 us; the launch traced here: 28.8 us
  Pallas kernels  26.7 us (92%)
  local copies, waits for them, and re-layouts  2.09 us (7%)
    pallas_call x1, Pallas kernels, shards(): pl.pallas_call(functools.partial(kernel, nr, nc), out_shape=jax.ShapeDtyp...  26.7 us
    unnamed x1, local copies, waits for them, and re-layouts  2.09 us

profile of v1, /device:TPU:1, one launch (start us, length us, event | category | flops | bytes accessed | tf_op | source)
XLA Modules:
  0.0 28.8 jit_solution(3626304690999497889)
XLA Ops:
  0.0 26.7 %shard_map.100 = f32[3,64,1024]{2,1,0:T(8,128)} custom-call(f32[3,64,1024]{2,1,0:T(8,128)} %res_h.1, f32[3,64,1024]{2,1,0:T(8,128)} %wts_h.1, bf16[3,64,1024]{2,1,0:T(8,128)(2,1)} %acc_h.1, bf16[3,64,1024]{2,1,0:T(8,128)(2,1)} %mob_h.1, f32[64,1024]{1,0:T(8,128)} %trans_h.1, bf16[9,64,1024]{2,1,0:T(8,128)(2,1)} %cell_h.1, bf16[1,8,128,128]{3,2,1,0:T(8,128)(2,1)} %pinv_h.1, ...), custom_call_target="tpu_custom_call" | custom-call | tf_op jit(solution)/shard_map/pallas_call | solution.py:307
  26.7 2.1 %copy.12 = f32[3,64,1024]{2,1,0:T(8,128)} copy(f32[3,64,1024]{2,1,0:T(8,128)} %shard_map.100) | data formatting | bytes 1572864

commit v2 on v1

v2 whole, which is shorter than its diff:
```python
import functools
import math

import jax
import jax.numpy as jnp
from jax import lax
from jax.experimental import pallas as pl
from jax.experimental.pallas import tpu as pltpu
from jax.sharding import PartitionSpec as P

H = 32
PR = 16
PC = 128
L = 128
TOP = 8
MESH = pl.DeviceIdType.MESH
F32 = jnp.float32
BF16 = jnp.bfloat16


def kernel(
    nr, nc,
    res_h, wts_h, acc_h, mob_h, trans_h, cell_h, pinv_h, ci_h, cnt_h, slot_h,
    out_ref,
    res_v, wts_v, acc_v, mob_v, tp_v, cell_v, pinv_v, ci_v, cnt_s, slot_v,
    rp_v, halo_v, ext_v, trow_s, trow_r, tcol_r, drow_s, drow_r, dcol_r, dp_v, cv_v, chr_v, chl_v,
    ps_v, tile_s, tile_r, corr_v,
    load_sem, send_sem, recv_sem, tile_send, tile_recv,
):
    rows = trans_h.shape[0]
    cols = trans_h.shape[1]
    nq = cols // L
    npr = rows // PR
    kmax = ci_h.shape[-1]
    pairs = nq // 2
    order = [pairs - 1] + list(range(pairs - 1))
    me_r = lax.axis_index("rows")
    me_c = lax.axis_index("cols")
    up = lax.rem(me_r + 1, nr)
    down = lax.rem(me_r + nr - 1, nr)
    right = lax.rem(me_c + 1, nc)
    left = lax.rem(me_c + nc - 1, nc)

    def load(src, dst, i):
        copy = pltpu.make_async_copy(src, dst, load_sem.at[i])
        copy.start()
        return copy

    rw = []
    for n, w in enumerate(order):
        span = pl.ds(w * 2 * L, 2 * L)
        rw.append((
            load(res_h.at[:, :, span], res_v.at[:, :, span], 2 * n),
            load(wts_h.at[:, :, span], wts_v.at[:, :, span], 2 * n + 1),
        ))
        if n == 0:
            load_t = load(trans_h, tp_v.at[pl.ds(TOP, rows), :], 8)
            load_ci = load(ci_h.at[0, 0], ci_v, 9)
            load_slot = load(slot_h, slot_v, 10)
            load_cnt = load(cnt_h, cnt_s, 11)
    load_p = load(pinv_h.at[0], pinv_v, 12)
    load_m = load(mob_h, mob_v, 13)
    load_a = load(acc_h, acc_v, 14)
    load_c = load(cell_h, cell_v, 15)

    barrier = pltpu.get_barrier_semaphore()
    for target in (up, down):
        pl.semaphore_signal(barrier, inc=1, device_id=(target, me_c), device_id_type=MESH)
    for k in range(1, nc):
        pl.semaphore_signal(
            barrier, inc=1, device_id=(me_r, lax.rem(me_c + k, nc)), device_id_type=MESH
        )

    sent = []

    def send(src, dst, i, device):
        copy = pltpu.make_async_remote_copy(
            src_ref=src, dst_ref=dst, send_sem=send_sem.at[i], recv_sem=recv_sem.at[i],
            device_id=device, device_id_type=MESH,
        )
        copy.start()
        sent.append(copy)
        return copy

    body = pl.ds(TOP, rows)
    first = pl.ds(0, L)
    last = pl.ds(cols - L, L)
    halos = []
    for n, w in enumerate(order):
        rw[n][0].wait()
        rw[n][1].wait()
        for q in (2 * w, 2 * w + 1):
            c = slice(q * L, (q + 1) * L)
            for p in range(npr):
                r = slice(p * PR, (p + 1) * PR)
                rp = res_v[0, r, c] * wts_v[0, r, c]
                rp = rp + res_v[1, r, c] * wts_v[1, r, c]
                rp = rp + res_v[2, r, c] * wts_v[2, r, c]
                rp_v[r, c] = rp
                ext_v[H + p * PR : H + (p + 1) * PR, c] = rp.astype(BF16)
                ps_v[p : p + 1, c] = jnp.sum(rp, axis=0, keepdims=True)
        if n == 0:
            pl.semaphore_wait(barrier, nc + 1)
        span = pl.ds(w * 2 * L, 2 * L)
        halos.append((
            send(rp_v.at[pl.ds(0, H), span], halo_v.at[1, :, span], 2 * n, (down, me_c)),
            send(rp_v.at[pl.ds(H, H), span], halo_v.at[0, :, span], 2 * n + 1, (up, me_c)),
        ))
        if n == 0:
            load_t.wait()
            trow_s[0] = tp_v[TOP : TOP + 1, :]
            trow_s[1] = tp_v[TOP + rows - 1 : TOP + rows, :]
            edge_t = [
                send(tp_v.at[body, first], tcol_r.at[1], 8, (me_r, left)),
                send(tp_v.at[body, last], tcol_r.at[0], 9, (me_r, right)),
                send(trow_s.at[0], trow_r.at[1], 10, (down, me_c)),
                send(trow_s.at[1], trow_r.at[0], 11, (up, me_c)),
            ]

    load_ci.wait()
    load_slot.wait()
    lane8 = lax.broadcasted_iota(jnp.int32, (8, L), 1)
    sub8 = lax.broadcasted_iota(jnp.int32, (8, L), 0)
    block = jnp.zeros((kmax, L), F32)
    own = ci_v[...]
    for j in range(kmax):
        block = block + jnp.where(lane8 == me_c * kmax + j, own[:, j : j + 1], 0.0)
    tile_s[0:8, :] = block
    tile_s[8:16, :] = jnp.zeros((8, L), F32)
    lane4 = lax.broadcasted_iota(jnp.int32, (npr, L), 1)
    slots = slot_v[...]
    tiles = jnp.zeros((npr, L), F32)
    hot = []
    for q in range(nq):
        sums = jnp.sum(ps_v[0:npr, q * L : (q + 1) * L], axis=1, keepdims=True)
        hit = lane4 == slots[:, q : q + 1]
        hot.append(hit)
        tiles = tiles + jnp.where(hit, sums, 0.0)
    tiles = jnp.sum(tiles, axis=0, keepdims=True) * (1.0 / math.sqrt(PR * PC))
    tile_s[8:9, :] = tiles
    tile_copies = []
    for k in range(1, nc):
        copy = pltpu.make_async_remote_copy(
            src_ref=tile_s, dst_ref=tile_r.at[k],
            send_sem=tile_send.at[k], recv_sem=tile_recv.at[k],
            device_id=(me_r, lax.rem(me_c + k, nc)), device_id_type=MESH,
        )
        copy.start()
        tile_copies.append(copy)

    for copy in edge_t:
        copy.wait_recv()
    tp_v[TOP - 1 : TOP, :] = trow_r[0]
    tp_v[TOP + rows : TOP + rows + 1, :] = trow_r[1]

    lane16 = lax.broadcasted_iota(jnp.int32, (PR, L), 1)
    is_last = lane16 == L - 1
    is_first = lane16 == 0

    def mean(a, b):
        return 2.0 * a * b / (a + b)

    for q in range(nq):
        c = slice(q * L, (q + 1) * L)
        low = mean(tp_v[TOP - 1 : TOP, c], tp_v[TOP : TOP + 1, c])
        cv_v[TOP - 1 : TOP, c] = jnp.where(me_r > 0, low, 0.0)
    for p in range(npr):
        r0 = TOP + p * PR
        r = slice(p * PR, (p + 1) * PR)
        blocks = [tcol_r[0, r, :]]
        blocks += [tp_v[r0 : r0 + PR, q * L : (q + 1) * L] for q in range(nq)]
        blocks += [tcol_r[1, r, :]]
        turned = [pltpu.roll(b, L - 1, 1) for b in blocks[1:]]
        before = None
        for q in range(nq + 1):
            here = blocks[q]
            if q == 0:
                near = turned[0]
            else:
                near = jnp.where(is_last, turned[q], turned[q - 1])
            face = mean(here, near)
            if q == 0:
                face = jnp.where(me_c > 0, face, 0.0)
            if q == nq:
                face = jnp.where(is_last & (me_c == nc - 1), 0.0, face)
            moved = pltpu.roll(face, 1, 1)
            if q > 0:
                c = slice((q - 1) * L, q * L)
                chr_v[r, c] = face
                chl_v[r, c] = jnp.where(is_first, before, moved)
                cv_v[r0 : r0 + PR, c] = mean(here, tp_v[r0 + 1 : r0 + PR + 1, c])
            before = moved
    for q in range(nq):
        c = slice(q * L, (q + 1) * L)
        r = slice(TOP + rows - 1, TOP + rows)
        cv_v[r, c] = jnp.where(me_r < nr - 1, cv_v[r, c], 0.0)

    load_p.wait()
    load_cnt.wait()
    row_e = lax.broadcasted_iota(jnp.int32, (H, L), 0)
    lo_count = jnp.where(me_r > 0, cnt_s[0, 0], 0)
    hi_count = jnp.where(me_r < nr - 1, cnt_s[0, 1], 0)

    for copy in tile_copies:
        copy.wait_recv()
    total = tile_s[8:16, :]
    for k in range(1, nc):
        total = total + tile_r[k, 8:16, :]
    total = total[0:1, :]
    coarse = jnp.zeros((8, L), F32)
    for k in range(nc):
        part = tile_s[0:8, :] if k == 0 else tile_r[k, 0:8, :]
        owner = lax.rem(me_c - k + nc, nc)
        value = jnp.sum(part * total, axis=1, keepdims=True)
        coarse = coarse + jnp.where(lane8 == owner * kmax + sub8, value, 0.0)
    coarse = jnp.sum(coarse, axis=0, keepdims=True)
    for q in range(nq):
        corr = jnp.sum(jnp.where(hot[q], coarse, 0.0), axis=1, keepdims=True)
        corr_v[0:npr, q * L : (q + 1) * L] = jnp.broadcast_to(corr, (npr, L))

    edge_c = []
    edge_r = []
    for n, w in enumerate(order):
        for copy in halos[n]:
            copy.wait_recv()
        for q in (2 * w, 2 * w + 1):
            c = slice(q * L, (q + 1) * L)
            low = jnp.where(row_e >= H - lo_count, halo_v[0, :, c], 0.0)
            high = jnp.where(row_e < hi_count, halo_v[1, :, c], 0.0)
            ext_v[0:H, c] = low.astype(BF16)
            ext_v[H + rows : 2 * H + rows, c] = high.astype(BF16)
            z = jnp.dot(pinv_v[q, H : H + rows, :], ext_v[:, c], preferred_element_type=F32)
            for p in range(npr):
                dp = z[p * PR : (p + 1) * PR, :] + corr_v[p : p + 1, c]
                dp_v[TOP + p * PR : TOP + (p + 1) * PR, c] = dp
                if p == 0:
                    drow_s[0, :, c] = dp[0:1, :]
                    dp_v[TOP - 1 : TOP, c] = dp[0:1, :]
                if p == npr - 1:
                    drow_s[1, :, c] = dp[PR - 1 : PR, :]
                    dp_v[TOP + rows : TOP + rows + 1, c] = dp[PR - 1 : PR, :]
        span = pl.ds(w * 2 * L, 2 * L)
        edge_r.append(send(drow_s.at[0, :, span], drow_r.at[1, :, span], 12 + 2 * n, (down, me_c)))
        edge_r.append(send(drow_s.at[1, :, span], drow_r.at[0, :, span], 13 + 2 * n, (up, me_c)))
        if w == pairs - 1:
            edge_c.append(send(dp_v.at[body, last], dcol_r.at[0], 20, (me_r, right)))
        if w == 0:
            edge_c.append(send(dp_v.at[body, first], dcol_r.at[1], 21, (me_r, left)))

    load_m.wait()
    load_a.wait()
    load_c.wait()

    def column(p, q):
        r0 = TOP + p * PR
        if q < 0:
            return dcol_r[0, p * PR : (p + 1) * PR, :]
        if q == nq:
            return dcol_r[1, p * PR : (p + 1) * PR, :]
        return dp_v[r0 : r0 + PR, q * L : (q + 1) * L]

    def finish(p, q):
        r0 = TOP + p * PR
        r = slice(p * PR, (p + 1) * PR)
        c = slice(q * L, (q + 1) * L)
        here = column(p, q)
        after = jnp.where(is_last, pltpu.roll(column(p, q + 1), L - 1, 1), pltpu.roll(here, L - 1, 1))
        prior = jnp.where(is_first, pltpu.roll(column(p, q - 1), 1, 1), pltpu.roll(here, 1, 1))
        flux = chr_v[r, c] * (here - after) + chl_v[r, c] * (here - prior)
        flux = flux + cv_v[r0 : r0 + PR, c] * (here - dp_v[r0 + 1 : r0 + PR + 1, c])
        flux = flux + cv_v[r0 - 1 : r0 + PR - 1, c] * (here - dp_v[r0 - 1 : r0 + PR - 1, c])
        r2 = [
            res_v[k, r, c]
            - (acc_v[k, r, c].astype(F32) * here + mob_v[k, r, c].astype(F32) * flux)
            for k in range(3)
        ]
        for k in range(3):
            u = cell_v[3 * k, r, c].astype(F32) * r2[0]
            u = u + cell_v[3 * k + 1, r, c].astype(F32) * r2[1]
            u = u + cell_v[3 * k + 2, r, c].astype(F32) * r2[2]
            if k == 0:
                u = u + here
            out_ref[k, r, c] = u

    for q in range(1, nq - 1):
        for p in range(npr):
            finish(p, q)
    for copy in edge_c:
        copy.wait_recv()
    for q in (0, nq - 1):
        for p in range(npr):
            finish(p, q)
    for copy in edge_r:
        copy.wait_recv()
    for q in range(nq):
        c = slice(q * L, (q + 1) * L)
        for e in range(2):
            r = slice(0, 8) if e == 0 else slice(rows - 8, rows)
            face = slice(TOP - 1, TOP) if e == 0 else slice(TOP + rows - 1, TOP + rows)
            mine = slice(TOP, TOP + 1) if e == 0 else slice(TOP + rows - 1, TOP + rows)
            extra = cv_v[face, c] * (dp_v[mine, c] - drow_r[e, :, c])
            extra = jnp.where(sub8 == (0 if e == 0 else 7), extra, 0.0)
            m = [mob_v[j, r, c].astype(F32) * extra for j in range(3)]
            for k in range(3):
                u = cell_v[3 * k, r, c].astype(F32) * m[0]
                u = u + cell_v[3 * k + 1, r, c].astype(F32) * m[1]
                u = u + cell_v[3 * k + 2, r, c].astype(F32) * m[2]
                out_ref[k, r, c] = out_ref[k, r, c] - u
    for copy in sent + tile_copies:
        copy.wait_send()


def shards(nr, nc, *args):
    residual, pinv = args[0], args[6]
    rows, cols = residual.shape[1:]
    groups = pinv.shape[1]
    e = rows + 2 * H
    hbm = pl.BlockSpec(memory_space=pl.ANY)
    vmem = pl.BlockSpec(memory_space=pltpu.VMEM)
    tall = rows + 2 * TOP
    scratch = [
        pltpu.VMEM((3, rows, cols), F32),
        pltpu.VMEM((3, rows, cols), F32),
        pltpu.VMEM((3, rows, cols), BF16),
        pltpu.VMEM((3, rows, cols), BF16),
        pltpu.VMEM((tall, cols), F32),
        pltpu.VMEM((9, rows, cols), BF16),
        pltpu.VMEM((groups, e, L), BF16),
        pltpu.VMEM(args[7].shape[2:], F32),
        pltpu.SMEM(args[8].shape, jnp.int32),
        pltpu.VMEM(args[9].shape, jnp.int32),
        pltpu.VMEM((rows, cols), F32),
        pltpu.VMEM((2, H, cols), F32),
        pltpu.VMEM((e, cols), BF16),
        pltpu.VMEM((2, 1, cols), F32),
        pltpu.VMEM((2, 1, cols), F32),
        pltpu.VMEM((2, rows, L), F32),
        pltpu.VMEM((2, 1, cols), F32),
        pltpu.VMEM((2, 1, cols), F32),
        pltpu.VMEM((2, rows, L), F32),
        pltpu.VMEM((tall, cols), F32),
        pltpu.VMEM((tall, cols), F32),
        pltpu.VMEM((rows, cols), F32),
        pltpu.VMEM((rows, cols), F32),
        pltpu.VMEM((8, cols), F32),
        pltpu.VMEM((16, L), F32),
        pltpu.VMEM((nc, 16, L), F32),
        pltpu.VMEM((8, cols), F32),
        pltpu.SemaphoreType.DMA((16,)),
        pltpu.SemaphoreType.DMA((22,)),
        pltpu.SemaphoreType.DMA((22,)),
        pltpu.SemaphoreType.DMA((nc,)),
        pltpu.SemaphoreType.DMA((nc,)),
    ]
    return pl.pallas_call(
        functools.partial(kernel, nr, nc),
        out_shape=pltpu.VMEM((3, rows, cols), F32),
        in_specs=[hbm] * 10,
        out_specs=vmem,
        scratch_shapes=scratch,
        compiler_params=pltpu.CompilerParams(
            collective_id=0, has_side_effects=True, vmem_limit_bytes=60 * 1024 * 1024
        ),
    )(*args)


def solution(mesh):
    in_specs = (
        P(None, "rows", "cols"),
        P(None, "rows", "cols"),
        P(None, "rows", "cols"),
        P(None, "rows", "cols"),
        P("rows", "cols"),
        P(None, "rows", "cols"),
        P("rows", "cols", None, None),
        P("rows", "cols", None, None),
        P("rows", None),
        P("rows", "cols"),
    )
    out_specs = P(None, "rows", "cols")
    body = functools.partial(shards, mesh.shape["rows"], mesh.shape["cols"])
    return jax.shard_map(body, mesh=mesh, in_specs=in_specs, out_specs=out_specs, check_vma=False)
```

time: 29 us -> 24.6 us (0.85)
  the two profiles are of different devices: /device:TPU:1 before, /device:TPU:24 now
where the time goes in v2:
time: 24.6 us; the launch traced here: 24.5 us
  Pallas kernels  23.6 us (96%)
  local copies, waits for them, and re-layouts  0.88 us (4%)
    pallas_call x1, Pallas kernels, shards(): pl.pallas_call(functools.partial(kernel, nr, nc), out_shape=pltpu.VMEM((3...  23.6 us
    unnamed x1, local copies, waits for them, and re-layouts  0.88 us

profile of v2, /device:TPU:24, one launch (start us, length us, event | category | flops | bytes accessed | tf_op | source)
XLA Modules:
  0.0 24.5 jit_solution(12358114254769123798)
XLA Ops:
  0.0 23.6 %shard_map.100 = f32[3,64,1024]{2,1,0:T(8,128)S(1)} custom-call(f32[3,64,1024]{2,1,0:T(8,128)} %res_h.1, f32[3,64,1024]{2,1,0:T(8,128)} %wts_h.1, bf16[3,64,1024]{2,1,0:T(8,128)(2,1)} %acc_h.1, bf16[3,64,1024]{2,1,0:T(8,128)(2,1)} %mob_h.1, f32[64,1024]{1,0:T(8,128)} %trans_h.1, bf16[9,64,1024]{2,1,0:T(8,128)(2,1)} %cell_h.1, ...), custom_call_target="tpu_custom_call" | custom-call | tf_op jit(solution)/shard_map/pallas_call | solution.py:355
  23.6 0.9 %copy.12 = f32[3,64,1024]{2,1,0:T(8,128)} copy(f32[3,64,1024]{2,1,0:T(8,128)S(1)} %shard_map.100) | data formatting | bytes 1572864

commit v3 on v2

--- a/solution.py
+++ b/solution.py
@@ -58,11 +58,6 @@
             load_ci = load(ci_h.at[0, 0], ci_v, 9)
             load_slot = load(slot_h, slot_v, 10)
             load_cnt = load(cnt_h, cnt_s, 11)
-    load_p = load(pinv_h.at[0], pinv_v, 12)
-    load_m = load(mob_h, mob_v, 13)
-    load_a = load(acc_h, acc_v, 14)
-    load_c = load(cell_h, cell_v, 15)
-
     barrier = pltpu.get_barrier_semaphore()
     for target in (up, down):
         pl.semaphore_signal(barrier, inc=1, device_id=(target, me_c), device_id_type=MESH)
@@ -117,6 +112,11 @@
                 send(trow_s.at[1], trow_r.at[0], 11, (up, me_c)),
             ]
 
+    load_p = load(pinv_h.at[0], pinv_v, 12)
+    load_m = load(mob_h, mob_v, 13)
+    load_a = load(acc_h, acc_v, 14)
+    load_c = load(cell_h, cell_v, 15)
+
     load_ci.wait()
     load_slot.wait()
     lane8 = lax.broadcasted_iota(jnp.int32, (8, L), 1)
@@ -308,6 +308,12 @@
                 out_ref[k, r, c] = out_ref[k, r, c] - u
     for copy in sent + tile_copies:
         copy.wait_send()
+
+
+def place(in_ref, out_ref, sem):
+    copy = pltpu.make_async_copy(in_ref, out_ref, sem.at[0])
+    copy.start()
+    copy.wait()
 
 
 def shards(nr, nc, *args):
@@ -352,7 +358,7 @@
         pltpu.SemaphoreType.DMA((nc,)),
         pltpu.SemaphoreType.DMA((nc,)),
     ]
-    return pl.pallas_call(
+    update = pl.pallas_call(
         functools.partial(kernel, nr, nc),
         out_shape=pltpu.VMEM((3, rows, cols), F32),
         in_specs=[hbm] * 10,
@@ -362,6 +368,14 @@
             collective_id=0, has_side_effects=True, vmem_limit_bytes=60 * 1024 * 1024
         ),
     )(*args)
+    return pl.pallas_call(
+        place,
+        out_shape=jax.ShapeDtypeStruct((3, rows, cols), F32),
+        in_specs=[pl.BlockSpec(memory_space=pltpu.VMEM)],
+        out_specs=pl.BlockSpec(memory_space=pl.ANY),
+        scratch_shapes=[pltpu.SemaphoreType.DMA((1,))],
+        compiler_params=pltpu.CompilerParams(vmem_limit_bytes=1024 * 1024),
+    )(update)
 
 
 def solution(mesh):

time: 24.6 us -> 24.6 us (level)
  Pallas kernels: 23.6 us -> 24.5 us
  local copies, waits for them, and re-layouts: 0.88 us -> 0 us
    pallas_call x0 -> x1, Pallas kernels: none -> 0.89 us  [shards(): pl.pallas_call(place, out_shape=jax.ShapeDtypeStruct((3, rows, cols), F32...]
    unnamed x1 -> x0, local copies, waits for them, and re-layouts: 0.88 us -> none
where the time goes in v3:
time: 24.6 us; the launch traced here: 24.5 us
  Pallas kernels  24.5 us (100%)
    pallas_call x1, Pallas kernels, shards(): pl.pallas_call(functools.partial(kernel, nr, nc), out_shape=pltpu.VMEM((3...  23.6 us
    pallas_call x1, Pallas kernels, shards(): pl.pallas_call(place, out_shape=jax.ShapeDtypeStruct((3, rows, cols), F32...  0.89 us

profile of v3, /device:TPU:24, one launch (start us, length us, event | category | flops | bytes accessed | tf_op | source)
XLA Modules:
  0.0 24.5 jit_solution(11145348596306166081)
XLA Ops:
  0.0 23.6 %shard_map.100.in_ref = f32[3,64,1024]{2,1,0:T(8,128)S(1)} custom-call(f32[3,64,1024]{2,1,0:T(8,128)} %res_h.1, f32[3,64,1024]{2,1,0:T(8,128)} %wts_h.1, bf16[3,64,1024]{2,1,0:T(8,128)(2,1)} %acc_h.1, bf16[3,64,1024]{2,1,0:T(8,128)(2,1)} %mob_h.1, f32[64,1024]{1,0:T(8,128)} %trans_h.1, bf16[9,64,1024]{2,1,0:T(8,128)(2,1)} %cell_h.1, ...), custom_call_target="tpu_custom_call" | custom-call | tf_op jit(solution)/shard_map/pallas_call | solution.py:361
  23.6 0.9 %shard_map.101 = f32[3,64,1024]{2,1,0:T(8,128)} custom-call(f32[3,64,1024]{2,1,0:T(8,128)S(1)} %shard_map.100.in_ref), custom_call_target="tpu_custom_call" | custom-call | tf_op jit(solution)/shard_map/pallas_call | solution.py:371

commit v4 on v3

--- a/solution.py
+++ b/solution.py
@@ -59,8 +59,14 @@
             load_slot = load(slot_h, slot_v, 10)
             load_cnt = load(cnt_h, cnt_s, 11)
     barrier = pltpu.get_barrier_semaphore()
-    for target in (up, down):
-        pl.semaphore_signal(barrier, inc=1, device_id=(target, me_c), device_id_type=MESH)
+    has_down = me_r > 0
+    has_up = me_r < nr - 1
+    has_left = me_c > 0
+    has_right = me_c < nc - 1
+    for target, there in ((up, has_up), (down, has_down)):
+        @pl.when(there)
+        def _():
+            pl.semaphore_signal(barrier, inc=1, device_id=(target, me_c), device_id_type=MESH)
     for k in range(1, nc):
         pl.semaphore_signal(
             barrier, inc=1, device_id=(me_r, lax.rem(me_c + k, nc)), device_id_type=MESH
@@ -68,14 +74,26 @@
 
     sent = []
 
-    def send(src, dst, i, device):
+    ways = {
+        "down": ((down, me_c), has_down, has_up),
+        "up": ((up, me_c), has_up, has_down),
+        "left": ((me_r, left), has_left, has_right),
+        "right": ((me_r, right), has_right, has_left),
+    }
+
+    def send(src, dst, i, way):
+        device, goes, comes = ways[way]
         copy = pltpu.make_async_remote_copy(
             src_ref=src, dst_ref=dst, send_sem=send_sem.at[i], recv_sem=recv_sem.at[i],
             device_id=device, device_id_type=MESH,
         )
-        copy.start()
-        sent.append(copy)
-        return copy
+        pl.when(goes)(copy.start)
+        sent.append((copy, goes))
+        return copy, comes
+
+    def arrive(copies):
+        for copy, comes in copies:
+            pl.when(comes)(copy.wait_recv)
 
     body = pl.ds(TOP, rows)
     first = pl.ds(0, L)
@@ -95,21 +113,21 @@
                 ext_v[H + p * PR : H + (p + 1) * PR, c] = rp.astype(BF16)
                 ps_v[p : p + 1, c] = jnp.sum(rp, axis=0, keepdims=True)
         if n == 0:
-            pl.semaphore_wait(barrier, nc + 1)
+            pl.semaphore_wait(barrier, nc - 1 + has_down.astype(jnp.int32) + has_up.astype(jnp.int32))
         span = pl.ds(w * 2 * L, 2 * L)
         halos.append((
-            send(rp_v.at[pl.ds(0, H), span], halo_v.at[1, :, span], 2 * n, (down, me_c)),
-            send(rp_v.at[pl.ds(H, H), span], halo_v.at[0, :, span], 2 * n + 1, (up, me_c)),
+            send(rp_v.at[pl.ds(0, H), span], halo_v.at[1, :, span], 2 * n, "down"),
+            send(rp_v.at[pl.ds(H, H), span], halo_v.at[0, :, span], 2 * n + 1, "up"),
         ))
         if n == 0:
             load_t.wait()
             trow_s[0] = tp_v[TOP : TOP + 1, :]
             trow_s[1] = tp_v[TOP + rows - 1 : TOP + rows, :]
             edge_t = [
-                send(tp_v.at[body, first], tcol_r.at[1], 8, (me_r, left)),
-                send(tp_v.at[body, last], tcol_r.at[0], 9, (me_r, right)),
-                send(trow_s.at[0], trow_r.at[1], 10, (down, me_c)),
-                send(trow_s.at[1], trow_r.at[0], 11, (up, me_c)),
+                send(tp_v.at[body, first], tcol_r.at[1], 8, "left"),
+                send(tp_v.at[body, last], tcol_r.at[0], 9, "right"),
+                send(trow_s.at[0], trow_r.at[1], 10, "down"),
+                send(trow_s.at[1], trow_r.at[0], 11, "up"),
             ]
 
     load_p = load(pinv_h.at[0], pinv_v, 12)
@@ -148,8 +166,16 @@
         copy.start()
         tile_copies.append(copy)
 
-    for copy in edge_t:
-        copy.wait_recv()
+    for i, row, col in ((0, has_down, has_left), (1, has_up, has_right)):
+        @pl.when(jnp.logical_not(row))
+        def _():
+            drow_r[i] = jnp.zeros(drow_r.shape[1:], F32)
+
+        @pl.when(jnp.logical_not(col))
+        def _():
+            dcol_r[i] = jnp.zeros(dcol_r.shape[1:], F32)
+
+    arrive(edge_t)
     tp_v[TOP - 1 : TOP, :] = trow_r[0]
     tp_v[TOP + rows : TOP + rows + 1, :] = trow_r[1]
 
@@ -221,8 +247,7 @@
     edge_c = []
     edge_r = []
     for n, w in enumerate(order):
-        for copy in halos[n]:
-            copy.wait_recv()
+        arrive(halos[n])
         for q in (2 * w, 2 * w + 1):
             c = slice(q * L, (q + 1) * L)
             low = jnp.where(row_e >= H - lo_count, halo_v[0, :, c], 0.0)
@@ -240,12 +265,12 @@
                     drow_s[1, :, c] = dp[PR - 1 : PR, :]
                     dp_v[TOP + rows : TOP + rows + 1, c] = dp[PR - 1 : PR, :]
         span = pl.ds(w * 2 * L, 2 * L)
-        edge_r.append(send(drow_s.at[0, :, span], drow_r.at[1, :, span], 12 + 2 * n, (down, me_c)))
-        edge_r.append(send(drow_s.at[1, :, span], drow_r.at[0, :, span], 13 + 2 * n, (up, me_c)))
+        edge_r.append(send(drow_s.at[0, :, span], drow_r.at[1, :, span], 12 + 2 * n, "down"))
+        edge_r.append(send(drow_s.at[1, :, span], drow_r.at[0, :, span], 13 + 2 * n, "up"))
         if w == pairs - 1:
-            edge_c.append(send(dp_v.at[body, last], dcol_r.at[0], 20, (me_r, right)))
+            edge_c.append(send(dp_v.at[body, last], dcol_r.at[0], 20, "right"))
         if w == 0:
-            edge_c.append(send(dp_v.at[body, first], dcol_r.at[1], 21, (me_r, left)))
+            edge_c.append(send(dp_v.at[body, first], dcol_r.at[1], 21, "left"))
 
     load_m.wait()
     load_a.wait()
@@ -285,13 +310,11 @@
     for q in range(1, nq - 1):
         for p in range(npr):
             finish(p, q)
-    for copy in edge_c:
-        copy.wait_recv()
+    arrive(edge_c)
     for q in (0, nq - 1):
         for p in range(npr):
             finish(p, q)
-    for copy in edge_r:
-        copy.wait_recv()
+    arrive(edge_r)
     for q in range(nq):
         c = slice(q * L, (q + 1) * L)
         for e in range(2):
@@ -306,7 +329,9 @@
                 u = u + cell_v[3 * k + 1, r, c].astype(F32) * m[1]
                 u = u + cell_v[3 * k + 2, r, c].astype(F32) * m[2]
                 out_ref[k, r, c] = out_ref[k, r, c] - u
-    for copy in sent + tile_copies:
+    for copy, goes in sent:
+        pl.when(goes)(copy.wait_send)
+    for copy in tile_copies:
         copy.wait_send()
 
 

time: 24.6 us -> 22.2 us (0.902)
  the two profiles are of different devices: /device:TPU:24 before, /device:TPU:6 now
where the time goes in v4:
time: 22.2 us; the launch traced here: 22 us
  Pallas kernels  22 us (99%)
    pallas_call x1, Pallas kernels, shards(): pl.pallas_call(functools.partial(kernel, nr, nc), out_shape=pltpu.VMEM((3...  21.1 us
    pallas_call x1, Pallas kernels, shards(): pl.pallas_call(place, out_shape=jax.ShapeDtypeStruct((3, rows, cols), F32...  0.89 us

profile of v4, /device:TPU:6, one launch (start us, length us, event | category | flops | bytes accessed | tf_op | source)
XLA Modules:
  0.0 22.0 jit_solution(5524280698178787818)
XLA Ops:
  0.0 21.1 %shard_map.100.in_ref = f32[3,64,1024]{2,1,0:T(8,128)S(1)} custom-call(f32[3,64,1024]{2,1,0:T(8,128)} %res_h.1, f32[3,64,1024]{2,1,0:T(8,128)} %wts_h.1, bf16[3,64,1024]{2,1,0:T(8,128)(2,1)} %acc_h.1, bf16[3,64,1024]{2,1,0:T(8,128)(2,1)} %mob_h.1, f32[64,1024]{1,0:T(8,128)} %trans_h.1, bf16[9,64,1024]{2,1,0:T(8,128)(2,1)} %cell_h.1, ...), custom_call_target="tpu_custom_call" | custom-call | tf_op jit(solution)/shard_map/pallas_call | solution.py:386
  21.1 0.9 %shard_map.101 = f32[3,64,1024]{2,1,0:T(8,128)} custom-call(f32[3,64,1024]{2,1,0:T(8,128)S(1)} %shard_map.100.in_ref), custom_call_target="tpu_custom_call" | custom-call | tf_op jit(solution)/shard_map/pallas_call | solution.py:396

commit v5 on v4

--- a/solution.py
+++ b/solution.py
@@ -24,7 +24,7 @@
     out_ref,
     res_v, wts_v, acc_v, mob_v, tp_v, cell_v, pinv_v, ci_v, cnt_s, slot_v,
     rp_v, halo_v, ext_v, trow_s, trow_r, tcol_r, drow_s, drow_r, dcol_r, dp_v, cv_v, chr_v, chl_v,
-    ps_v, tile_s, tile_r, corr_v,
+    ps_v, tile_s, tile_r, corr_v, w_s, w_r, lo_v, add_v,
     load_sem, send_sem, recv_sem, tile_send, tile_recv,
 ):
     rows = trans_h.shape[0]
@@ -58,6 +58,8 @@
             load_ci = load(ci_h.at[0, 0], ci_v, 9)
             load_slot = load(slot_h, slot_v, 10)
             load_cnt = load(cnt_h, cnt_s, 11)
+    load_p = load(pinv_h.at[0], pinv_v, 12)
+
     barrier = pltpu.get_barrier_semaphore()
     has_down = me_r > 0
     has_up = me_r < nr - 1
@@ -98,6 +100,7 @@
     body = pl.ds(TOP, rows)
     first = pl.ds(0, L)
     last = pl.ds(cols - L, L)
+    lane8 = lax.broadcasted_iota(jnp.int32, (8, L), 1)
     halos = []
     for n, w in enumerate(order):
         rw[n][0].wait()
@@ -129,15 +132,29 @@
                 send(trow_s.at[0], trow_r.at[1], 10, "down"),
                 send(trow_s.at[1], trow_r.at[0], 11, "up"),
             ]
-
-    load_p = load(pinv_h.at[0], pinv_v, 12)
+        if n == 1:
+            load_p.wait()
+            load_cnt.wait()
+            lo_count = jnp.where(me_r > 0, cnt_s[0, 0], 0)
+            hi_count = jnp.where(me_r < nr - 1, cnt_s[0, 1], 0)
+            for q in range(nq):
+                w_s[0, q : q + 1, :] = pinv_v[q, H : H + PR, :].astype(F32)[0:1, :]
+                w_s[1, q : q + 1, :] = pinv_v[q, H + rows - PR : H + rows, :].astype(F32)[PR - 1 : PR, :]
+            below = (lane8 < H) & (lane8 >= H - lo_count)
+            above = (lane8 >= H + rows) & (lane8 < H + rows + hi_count)
+            w_s[0] = pltpu.roll(jnp.where(below, w_s[0], 0.0), H, 1)
+            w_s[1] = pltpu.roll(jnp.where(above, w_s[1], 0.0), H, 1)
+            edge_w = [
+                send(w_s.at[1], w_r.at[0], 23, "up"),
+                send(w_s.at[0], w_r.at[1], 22, "down"),
+            ]
+
     load_m = load(mob_h, mob_v, 13)
     load_a = load(acc_h, acc_v, 14)
     load_c = load(cell_h, cell_v, 15)
 
     load_ci.wait()
     load_slot.wait()
-    lane8 = lax.broadcasted_iota(jnp.int32, (8, L), 1)
     sub8 = lax.broadcasted_iota(jnp.int32, (8, L), 0)
     block = jnp.zeros((kmax, L), F32)
     own = ci_v[...]
@@ -170,6 +187,7 @@
         @pl.when(jnp.logical_not(row))
         def _():
             drow_r[i] = jnp.zeros(drow_r.shape[1:], F32)
+            w_r[i] = jnp.zeros(w_r.shape[1:], F32)
 
         @pl.when(jnp.logical_not(col))
         def _():
@@ -221,11 +239,7 @@
         r = slice(TOP + rows - 1, TOP + rows)
         cv_v[r, c] = jnp.where(me_r < nr - 1, cv_v[r, c], 0.0)
 
-    load_p.wait()
-    load_cnt.wait()
     row_e = lax.broadcasted_iota(jnp.int32, (H, L), 0)
-    lo_count = jnp.where(me_r > 0, cnt_s[0, 0], 0)
-    hi_count = jnp.where(me_r < nr - 1, cnt_s[0, 1], 0)
 
     for copy in tile_copies:
         copy.wait_recv()
@@ -246,27 +260,53 @@
 
     edge_c = []
     edge_r = []
+
+    def own_part(side):
+        arrive(edge_w[side : side + 1])
+        lhs = w_r[side].astype(BF16)[:, 0:rows]
+        for q in range(nq):
+            c = slice(q * L, (q + 1) * L)
+            part = jnp.dot(lhs, ext_v[H : H + rows, c], preferred_element_type=F32)
+            add_v[side, :, c] = part[q : q + 1, :]
+
     for n, w in enumerate(order):
-        arrive(halos[n])
+        if n == pairs - 1:
+            own_part(0)
+        arrive(halos[n][1:2])
         for q in (2 * w, 2 * w + 1):
             c = slice(q * L, (q + 1) * L)
             low = jnp.where(row_e >= H - lo_count, halo_v[0, :, c], 0.0)
+            ext_v[0:H, c] = low.astype(BF16)
+            top = jnp.dot(
+                pinv_v[q, H + rows - PR : H + rows, :][:, 0 : H + rows], ext_v[0 : H + rows, c],
+                preferred_element_type=F32,
+            )
+            drow_s[1, :, c] = top[PR - 1 : PR, :] + corr_v[npr - 1 : npr, c]
+            low = jnp.dot(
+                pinv_v[q, H : H + PR, :][:, 0:H], ext_v[0:H, c], preferred_element_type=F32
+            )
+            lo_v[0:1, c] = low[0:1, :]
+        span = pl.ds(w * 2 * L, 2 * L)
+        edge_r.append(send(drow_s.at[1, :, span], drow_r.at[0, :, span], 13 + 2 * n, "up"))
+    for n, w in enumerate(order):
+        if n == pairs - 1:
+            own_part(1)
+        arrive(halos[n][0:1])
+        for q in (2 * w, 2 * w + 1):
+            c = slice(q * L, (q + 1) * L)
             high = jnp.where(row_e < hi_count, halo_v[1, :, c], 0.0)
-            ext_v[0:H, c] = low.astype(BF16)
             ext_v[H + rows : 2 * H + rows, c] = high.astype(BF16)
             z = jnp.dot(pinv_v[q, H : H + rows, :], ext_v[:, c], preferred_element_type=F32)
             for p in range(npr):
                 dp = z[p * PR : (p + 1) * PR, :] + corr_v[p : p + 1, c]
                 dp_v[TOP + p * PR : TOP + (p + 1) * PR, c] = dp
                 if p == 0:
-                    drow_s[0, :, c] = dp[0:1, :]
+                    drow_s[0, :, c] = dp[0:1, :] - lo_v[0:1, c]
                     dp_v[TOP - 1 : TOP, c] = dp[0:1, :]
                 if p == npr - 1:
-                    drow_s[1, :, c] = dp[PR - 1 : PR, :]
                     dp_v[TOP + rows : TOP + rows + 1, c] = dp[PR - 1 : PR, :]
         span = pl.ds(w * 2 * L, 2 * L)
         edge_r.append(send(drow_s.at[0, :, span], drow_r.at[1, :, span], 12 + 2 * n, "down"))
-        edge_r.append(send(drow_s.at[1, :, span], drow_r.at[0, :, span], 13 + 2 * n, "up"))
         if w == pairs - 1:
             edge_c.append(send(dp_v.at[body, last], dcol_r.at[0], 20, "right"))
         if w == 0:
@@ -321,7 +361,7 @@
             r = slice(0, 8) if e == 0 else slice(rows - 8, rows)
             face = slice(TOP - 1, TOP) if e == 0 else slice(TOP + rows - 1, TOP + rows)
             mine = slice(TOP, TOP + 1) if e == 0 else slice(TOP + rows - 1, TOP + rows)
-            extra = cv_v[face, c] * (dp_v[mine, c] - drow_r[e, :, c])
+            extra = cv_v[face, c] * (dp_v[mine, c] - (drow_r[e, :, c] + add_v[e, :, c]))
             extra = jnp.where(sub8 == (0 if e == 0 else 7), extra, 0.0)
             m = [mob_v[j, r, c].astype(F32) * extra for j in range(3)]
             for k in range(3):
@@ -377,9 +417,13 @@
         pltpu.VMEM((16, L), F32),
         pltpu.VMEM((nc, 16, L), F32),
         pltpu.VMEM((8, cols), F32),
+        pltpu.VMEM((2, 8, L), F32),
+        pltpu.VMEM((2, 8, L), F32),
+        pltpu.VMEM((8, cols), F32),
+        pltpu.VMEM((2, 1, cols), F32),
         pltpu.SemaphoreType.DMA((16,)),
-        pltpu.SemaphoreType.DMA((22,)),
-        pltpu.SemaphoreType.DMA((22,)),
+        pltpu.SemaphoreType.DMA((24,)),
+        pltpu.SemaphoreType.DMA((24,)),
         pltpu.SemaphoreType.DMA((nc,)),
         pltpu.SemaphoreType.DMA((nc,)),
     ]

time: 22.2 us -> 22.8 us (1.027)
  the two profiles are of different devices: /device:TPU:6 before, /device:TPU:7 now
where the time goes in v5:
time: 22.8 us; the launch traced here: 22.7 us
  Pallas kernels  22.7 us (100%)
    pallas_call x1, Pallas kernels, shards(): pl.pallas_call(functools.partial(kernel, nr, nc), out_shape=pltpu.VMEM((3...  21.8 us
    pallas_call x1, Pallas kernels, shards(): pl.pallas_call(place, out_shape=jax.ShapeDtypeStruct((3, rows, cols), F32...  0.89 us

profile of v5, /device:TPU:7, one launch (start us, length us, event | category | flops | bytes accessed | tf_op | source)
XLA Modules:
  0.0 22.7 jit_solution(9499652397432595305)
XLA Ops:
  0.0 21.8 %shard_map.100.in_ref = f32[3,64,1024]{2,1,0:T(8,128)S(1)} custom-call(f32[3,64,1024]{2,1,0:T(8,128)} %res_h.1, f32[3,64,1024]{2,1,0:T(8,128)} %wts_h.1, bf16[3,64,1024]{2,1,0:T(8,128)(2,1)} %acc_h.1, bf16[3,64,1024]{2,1,0:T(8,128)(2,1)} %mob_h.1, f32[64,1024]{1,0:T(8,128)} %trans_h.1, bf16[9,64,1024]{2,1,0:T(8,128)(2,1)} %cell_h.1, ...), custom_call_target="tpu_custom_call" | custom-call | tf_op jit(solution)/shard_map/pallas_call | solution.py:430
  21.8 0.9 %shard_map.101 = f32[3,64,1024]{2,1,0:T(8,128)} custom-call(f32[3,64,1024]{2,1,0:T(8,128)S(1)} %shard_map.100.in_ref), custom_call_target="tpu_custom_call" | custom-call | tf_op jit(solution)/shard_map/pallas_call | solution.py:440

commit v6 on v4

--- a/solution.py
+++ b/solution.py
@@ -244,6 +244,37 @@
         corr = jnp.sum(jnp.where(hot[q], coarse, 0.0), axis=1, keepdims=True)
         corr_v[0:npr, q * L : (q + 1) * L] = jnp.broadcast_to(corr, (npr, L))
 
+    def column(p, q):
+        r0 = TOP + p * PR
+        if q < 0:
+            return dcol_r[0, p * PR : (p + 1) * PR, :]
+        if q == nq:
+            return dcol_r[1, p * PR : (p + 1) * PR, :]
+        return dp_v[r0 : r0 + PR, q * L : (q + 1) * L]
+
+    def finish(p, q):
+        r0 = TOP + p * PR
+        r = slice(p * PR, (p + 1) * PR)
+        c = slice(q * L, (q + 1) * L)
+        here = column(p, q)
+        after = jnp.where(is_last, pltpu.roll(column(p, q + 1), L - 1, 1), pltpu.roll(here, L - 1, 1))
+        prior = jnp.where(is_first, pltpu.roll(column(p, q - 1), 1, 1), pltpu.roll(here, 1, 1))
+        flux = chr_v[r, c] * (here - after) + chl_v[r, c] * (here - prior)
+        flux = flux + cv_v[r0 : r0 + PR, c] * (here - dp_v[r0 + 1 : r0 + PR + 1, c])
+        flux = flux + cv_v[r0 - 1 : r0 + PR - 1, c] * (here - dp_v[r0 - 1 : r0 + PR - 1, c])
+        r2 = [
+            res_v[k, r, c]
+            - (acc_v[k, r, c].astype(F32) * here + mob_v[k, r, c].astype(F32) * flux)
+            for k in range(3)
+        ]
+        for k in range(3):
+            u = cell_v[3 * k, r, c].astype(F32) * r2[0]
+            u = u + cell_v[3 * k + 1, r, c].astype(F32) * r2[1]
+            u = u + cell_v[3 * k + 2, r, c].astype(F32) * r2[2]
+            if k == 0:
+                u = u + here
+            out_ref[k, r, c] = u
+
     edge_c = []
     edge_r = []
     for n, w in enumerate(order):
@@ -271,43 +302,15 @@
             edge_c.append(send(dp_v.at[body, last], dcol_r.at[0], 20, "right"))
         if w == 0:
             edge_c.append(send(dp_v.at[body, first], dcol_r.at[1], 21, "left"))
-
-    load_m.wait()
-    load_a.wait()
-    load_c.wait()
-
-    def column(p, q):
-        r0 = TOP + p * PR
-        if q < 0:
-            return dcol_r[0, p * PR : (p + 1) * PR, :]
-        if q == nq:
-            return dcol_r[1, p * PR : (p + 1) * PR, :]
-        return dp_v[r0 : r0 + PR, q * L : (q + 1) * L]
-
-    def finish(p, q):
-        r0 = TOP + p * PR
-        r = slice(p * PR, (p + 1) * PR)
-        c = slice(q * L, (q + 1) * L)
-        here = column(p, q)
-        after = jnp.where(is_last, pltpu.roll(column(p, q + 1), L - 1, 1), pltpu.roll(here, L - 1, 1))
-        prior = jnp.where(is_first, pltpu.roll(column(p, q - 1), 1, 1), pltpu.roll(here, 1, 1))
-        flux = chr_v[r, c] * (here - after) + chl_v[r, c] * (here - prior)
-        flux = flux + cv_v[r0 : r0 + PR, c] * (here - dp_v[r0 + 1 : r0 + PR + 1, c])
-        flux = flux + cv_v[r0 - 1 : r0 + PR - 1, c] * (here - dp_v[r0 - 1 : r0 + PR - 1, c])
-        r2 = [
-            res_v[k, r, c]
-            - (acc_v[k, r, c].astype(F32) * here + mob_v[k, r, c].astype(F32) * flux)
-            for k in range(3)
-        ]
-        for k in range(3):
-            u = cell_v[3 * k, r, c].astype(F32) * r2[0]
-            u = u + cell_v[3 * k + 1, r, c].astype(F32) * r2[1]
-            u = u + cell_v[3 * k + 2, r, c].astype(F32) * r2[2]
-            if k == 0:
-                u = u + here
-            out_ref[k, r, c] = u
-
-    for q in range(1, nq - 1):
+        if n == pairs - 2:
+            load_m.wait()
+            load_a.wait()
+            load_c.wait()
+            for q in range(1, nq - 5):
+                for p in range(npr):
+                    finish(p, q)
+
+    for q in range(nq - 5, nq - 1):
         for p in range(npr):
             finish(p, q)
     arrive(edge_c)
@@ -336,9 +339,16 @@
 
 
 def place(in_ref, out_ref, sem):
-    copy = pltpu.make_async_copy(in_ref, out_ref, sem.at[0])
-    copy.start()
-    copy.wait()
+    step = in_ref.shape[1] // 4
+    copies = []
+    for k in range(in_ref.shape[0]):
+        for p in range(4):
+            part = (k, pl.ds(p * step, step))
+            copies.append(pltpu.make_async_copy(in_ref.at[part], out_ref.at[part], sem.at[4 * k + p]))
+    for copy in copies:
+        copy.start()
+    for copy in copies:
+        copy.wait()
 
 
 def shards(nr, nc, *args):
@@ -398,7 +408,7 @@
         out_shape=jax.ShapeDtypeStruct((3, rows, cols), F32),
         in_specs=[pl.BlockSpec(memory_space=pltpu.VMEM)],
         out_specs=pl.BlockSpec(memory_space=pl.ANY),
-        scratch_shapes=[pltpu.SemaphoreType.DMA((1,))],
+        scratch_shapes=[pltpu.SemaphoreType.DMA((12,))],
         compiler_params=pltpu.CompilerParams(vmem_limit_bytes=1024 * 1024),
     )(update)
 

time: 22.2 us -> 22.3 us (level)
  no operation moved by 1% of the time
where the time goes in v6:
time: 22.3 us; the launch traced here: 22.1 us
  Pallas kernels  22.1 us (99%)
    pallas_call x1, Pallas kernels, shards(): pl.pallas_call(functools.partial(kernel, nr, nc), out_shape=pltpu.VMEM((3...  21.1 us
    pallas_call x1, Pallas kernels, shards(): pl.pallas_call(place, out_shape=jax.ShapeDtypeStruct((3, rows, cols), F32...  0.97 us

profile of v6, /device:TPU:6, one launch (start us, length us, event | category | flops | bytes accessed | tf_op | source)
XLA Modules:
  0.0 22.1 jit_solution(16109282768334493701)
XLA Ops:
  0.0 21.1 %shard_map.100.in_ref = f32[3,64,1024]{2,1,0:T(8,128)S(1)} custom-call(f32[3,64,1024]{2,1,0:T(8,128)} %res_h.1, f32[3,64,1024]{2,1,0:T(8,128)} %wts_h.1, bf16[3,64,1024]{2,1,0:T(8,128)(2,1)} %acc_h.1, bf16[3,64,1024]{2,1,0:T(8,128)(2,1)} %mob_h.1, f32[64,1024]{1,0:T(8,128)} %trans_h.1, bf16[9,64,1024]{2,1,0:T(8,128)(2,1)} %cell_h.1, ...), custom_call_target="tpu_custom_call" | custom-call | tf_op jit(solution)/shard_map/pallas_call | solution.py:396
  21.1 1.0 %shard_map.101 = f32[3,64,1024]{2,1,0:T(8,128)} custom-call(f32[3,64,1024]{2,1,0:T(8,128)S(1)} %shard_map.100.in_ref), custom_call_target="tpu_custom_call" | custom-call | tf_op jit(solution)/shard_map/pallas_call | solution.py:406

commit v7 on v6

--- a/solution.py
+++ b/solution.py
@@ -46,6 +46,16 @@
         copy.start()
         return copy
 
+    barrier = pltpu.get_barrier_semaphore()
+    has_down = me_r > 0
+    has_up = me_r < nr - 1
+    has_left = me_c > 0
+    has_right = me_c < nc - 1
+    for target, there in ((up, has_up), (down, has_down)):
+        @pl.when(there)
+        def _():
+            pl.semaphore_signal(barrier, inc=1, device_id=(target, me_c), device_id_type=MESH)
+
     rw = []
     for n, w in enumerate(order):
         span = pl.ds(w * 2 * L, 2 * L)
@@ -58,15 +68,6 @@
             load_ci = load(ci_h.at[0, 0], ci_v, 9)
             load_slot = load(slot_h, slot_v, 10)
             load_cnt = load(cnt_h, cnt_s, 11)
-    barrier = pltpu.get_barrier_semaphore()
-    has_down = me_r > 0
-    has_up = me_r < nr - 1
-    has_left = me_c > 0
-    has_right = me_c < nc - 1
-    for target, there in ((up, has_up), (down, has_down)):
-        @pl.when(there)
-        def _():
-            pl.semaphore_signal(barrier, inc=1, device_id=(target, me_c), device_id_type=MESH)
     for k in range(1, nc):
         pl.semaphore_signal(
             barrier, inc=1, device_id=(me_r, lax.rem(me_c + k, nc)), device_id_type=MESH
@@ -339,16 +340,9 @@
 
 
 def place(in_ref, out_ref, sem):
-    step = in_ref.shape[1] // 4
-    copies = []
-    for k in range(in_ref.shape[0]):
-        for p in range(4):
-            part = (k, pl.ds(p * step, step))
-            copies.append(pltpu.make_async_copy(in_ref.at[part], out_ref.at[part], sem.at[4 * k + p]))
-    for copy in copies:
-        copy.start()
-    for copy in copies:
-        copy.wait()
+    copy = pltpu.make_async_copy(in_ref, out_ref, sem.at[0])
+    copy.start()
+    copy.wait()
 
 
 def shards(nr, nc, *args):
@@ -408,7 +402,7 @@
         out_shape=jax.ShapeDtypeStruct((3, rows, cols), F32),
         in_specs=[pl.BlockSpec(memory_space=pltpu.VMEM)],
         out_specs=pl.BlockSpec(memory_space=pl.ANY),
-        scratch_shapes=[pltpu.SemaphoreType.DMA((12,))],
+        scratch_shapes=[pltpu.SemaphoreType.DMA((1,))],
         compiler_params=pltpu.CompilerParams(vmem_limit_bytes=1024 * 1024),
     )(update)
 

time: 22.3 us -> 22.2 us (level)
  no operation moved by 1% of the time
where the time goes in v7:
time: 22.2 us; the launch traced here: 22 us
  Pallas kernels  22 us (99%)
    pallas_call x1, Pallas kernels, shards(): pl.pallas_call(functools.partial(kernel, nr, nc), out_shape=pltpu.VMEM((3...  21.1 us
    pallas_call x1, Pallas kernels, shards(): pl.pallas_call(place, out_shape=jax.ShapeDtypeStruct((3, rows, cols), F32...  0.89 us

profile of v7, /device:TPU:6, one launch (start us, length us, event | category | flops | bytes accessed | tf_op | source)
XLA Modules:
  0.0 22.0 jit_solution(15208287000663202075)
XLA Ops:
  0.0 21.1 %shard_map.100.in_ref = f32[3,64,1024]{2,1,0:T(8,128)S(1)} custom-call(f32[3,64,1024]{2,1,0:T(8,128)} %res_h.1, f32[3,64,1024]{2,1,0:T(8,128)} %wts_h.1, bf16[3,64,1024]{2,1,0:T(8,128)(2,1)} %acc_h.1, bf16[3,64,1024]{2,1,0:T(8,128)(2,1)} %mob_h.1, f32[64,1024]{1,0:T(8,128)} %trans_h.1, bf16[9,64,1024]{2,1,0:T(8,128)(2,1)} %cell_h.1, ...), custom_call_target="tpu_custom_call" | custom-call | tf_op jit(solution)/shard_map/pallas_call | solution.py:390
  21.1 0.9 %shard_map.101 = f32[3,64,1024]{2,1,0:T(8,128)} custom-call(f32[3,64,1024]{2,1,0:T(8,128)S(1)} %shard_map.100.in_ref), custom_call_target="tpu_custom_call" | custom-call | tf_op jit(solution)/shard_map/pallas_call | solution.py:400
